TPU v7x, 32 devices: a whole 2x2x4 slice. The times are simulated.
32 devices in a mesh: wide: 8 (over y, x, core), narrow: 4 (over z).
Axes of the slice: x: 2, y: 2, z: 4, core: 2. Of those that a mesh axis runs over, the one named last changes fastest.
Arguments:
- tokens: bfloat16 [16384, 768], P(('wide', 'narrow')), may hold values from -6 to 6
- noise: int32 [16384], P(('wide', 'narrow')), may hold values 0 or 1
- seq_lengths: int32 [8, 4], P('wide'), may hold values from 0 to 2048, as said below
- ln1_gain: float32 [768], replicated, may hold values from 0.25 to 1.75
- ln1_bias: float32 [768], replicated, may hold values from -3 to 3
- qkv_weight: bfloat16 [3, 768, 768], P(None, None, 'narrow'), may hold values from -0.21875 to 0.21875
- out_weight: bfloat16 [768, 768], P('narrow'), may hold values from -3 to 3
- ln2_gain: float32 [768], replicated, may hold values from 0.25 to 1.75
- ln2_bias: float32 [768], replicated, may hold values from -3 to 3
- up_weight: bfloat16 [768, 3072], P(None, 'narrow'), may hold values from -0.21875 to 0.21875
- up_bias: float32 [3072], P('narrow'), may hold values from -4 to 4
- down_weight: bfloat16 [3072, 768], P('narrow'), may hold values from -0.109375 to 0.109375
- down_bias: float32 [768], replicated, may hold values from -3 to 3
- mask_vector: float32 [768], replicated, may hold values from -4 to 4
- cotangent: bfloat16 [2, 16384, 768], P(None, ('wide', 'narrow')), may hold values from -6 to 6
Outputs:
- output: bfloat16 [2, 16384, 768], P(None, ('wide', 'narrow'))
- d_tokens: bfloat16 [16384, 768], P(('wide', 'narrow'))
- d_ln1_gain: float32 [768], replicated
- d_ln1_bias: float32 [768], replicated
- d_qkv_weight: float32 [3, 768, 768], P(None, 'wide', 'narrow')
- d_out_weight: float32 [768, 768], P('narrow', 'wide')
- d_ln2_gain: float32 [768], replicated
- d_ln2_bias: float32 [768], replicated
- d_up_weight: float32 [768, 3072], P('wide', 'narrow')
- d_up_bias: float32 [3072], P(('narrow', 'wide'))
- d_down_weight: float32 [3072, 768], P('narrow', 'wide')
- d_down_bias: float32 [768], replicated
- d_mask_vector: float32 [768], replicated
Inputs may be any that keep to these rules, and one draw needn't show every extreme that they name: `seq_lengths`: row w lists the sequences packed on index w of wide in order; every length is a multiple of 16 and a row sums to 2048. A quarter of the rows hold one sequence of 2048 tokens followed by zeros; the others hold four sequences, each at least 1 token long.
All inputs are finite; a program needn't handle non-finite values. No bound on the sum of `noise` on one device may be relied on, other than what follows from the above.
Results may differ from a plain program's by a relative error of at most 0.019.
Values may be sent and summed in bfloat16 or wider, within the bound.
No kernel may reach another device: no remote copies, remote signals or barrier semaphores. Data moves between devices by JAX's collectives and lax.ppermute only.
A program may use at most 256 MiB of HBM per device.

v0:
```python
import math
import jax
import jax.numpy as jnp
from jax import lax
from jax.sharding import PartitionSpec as P

HEAD = 64
BLOCK = 16
EPS = 1e-05


def layer_norm(values, gain, shift):
    center = values - jnp.mean(values, axis=-1, keepdims=True)
    spread = jnp.mean(center * center, axis=-1, keepdims=True)
    return center * lax.rsqrt(spread + EPS) * gain + shift


def gelu_tanh(values):
    return jax.nn.gelu(values, approximate=True)


def rotate(values, cosines, sines):
    half = values.shape[-1] // 2
    turned = jnp.concatenate([-values[..., half:], values[..., :half]], axis=-1)
    return values * cosines + turned * sines


def angle_tables(positions, head):
    index_f = jnp.arange(head // 2).astype(jnp.float32)
    freqs = jnp.exp(index_f * (-2.0 * math.log(10000.0) / head))
    angles = positions.astype(jnp.float32)[:, None] * freqs[None, :]
    cosines = jnp.concatenate([jnp.cos(angles), jnp.cos(angles)], axis=-1)[:, None, :]
    sines = jnp.concatenate([jnp.sin(angles), jnp.sin(angles)], axis=-1)[:, None, :]
    return (cosines, sines)


def token_meta(lengths_row, count, block):
    ends = jnp.cumsum(lengths_row)
    starts = ends - lengths_row
    places = jnp.arange(count)
    seq_id = jnp.sum((places[:, None] >= ends[None, :]).astype(jnp.int32), axis=1)
    slot_ids = jnp.arange(lengths_row.shape[0])
    first = jnp.sum(jnp.where(seq_id[:, None] == slot_ids[None, :], starts[None, :], 0), axis=1)
    return (seq_id, places - first, places // block)


def allowed_pairs(q_seq, q_blk, q_copy, k_seq, k_blk, k_copy):
    same = q_seq[:, None] == k_seq[None, :]
    q_b = q_blk[:, None]
    k_b = k_blk[None, :]
    q_noisy = q_copy[:, None] == 0
    k_noisy = k_copy[None, :] == 0
    rule = jnp.where(
        q_noisy,
        jnp.where(k_noisy, q_b == k_b, k_b < q_b),
        jnp.logical_and(jnp.logical_not(k_noisy), k_b <= q_b),
    )
    return jnp.logical_and(same, rule)


def inner_rows(left, right):
    return lax.dot_general(
        left, right, (((0,), (0,)), ((), ())), preferred_element_type=jnp.float32
    )


def times_trans(left, right):
    return lax.dot_general(
        left, right, (((1,), (1,)), ((), ())), preferred_element_type=jnp.float32
    )


def per_device(
    tokens,
    noise,
    seq_lengths,
    ln1_gain,
    ln1_bias,
    qkv_weight,
    out_weight,
    ln2_gain,
    ln2_bias,
    up_weight,
    up_bias,
    down_weight,
    down_bias,
    mask_vector,
    cotangent,
):
    f32 = jnp.float32
    bf16 = jnp.bfloat16
    rows_dev, width = tokens.shape
    group_rows = rows_dev * lax.axis_size("narrow")
    count = 2 * group_rows
    local_width = qkv_weight.shape[2]
    heads_dev = local_width // HEAD
    scale = 1.0 / math.sqrt(HEAD)
    width_q = min(512, count)
    count_b = count // width_q
    clean = tokens.astype(f32)
    noisy = jnp.where(noise[:, None] == 1, mask_vector[None, :], clean)
    resid = jnp.stack([noisy, clean])
    normed1, norm1_pull = jax.vjp(layer_norm, resid, ln1_gain, ln1_bias)
    a_all = lax.all_gather(normed1.astype(bf16), "narrow", axis=1, tiled=True).reshape(count, width)
    seq_id, pos, blk = token_meta(seq_lengths[0], group_rows, BLOCK)
    seq2 = jnp.concatenate([seq_id, seq_id])
    pos2 = jnp.concatenate([pos, pos])
    blk2 = jnp.concatenate([blk, blk])
    copy2 = jnp.concatenate(
        [jnp.zeros((group_rows,), jnp.int32), jnp.ones((group_rows,), jnp.int32)]
    )
    cosines, sines = angle_tables(pos2, HEAD)

    def turn(values):
        return rotate(values, cosines, sines)

    q_pre = jnp.dot(a_all, qkv_weight[0], preferred_element_type=f32).reshape(
        count, heads_dev, HEAD
    )
    k_pre = jnp.dot(a_all, qkv_weight[1], preferred_element_type=f32).reshape(
        count, heads_dev, HEAD
    )
    q_rot, q_pull = jax.vjp(turn, q_pre)
    k_rot, k_pull = jax.vjp(turn, k_pre)
    queries = q_rot.astype(bf16)
    keys = k_rot.astype(bf16)
    values = (
        jnp.dot(a_all, qkv_weight[2], preferred_element_type=f32)
        .astype(bf16)
        .reshape(count, heads_dev, HEAD)
    )
    query_blocks = queries.reshape(count_b, width_q, heads_dev, HEAD)
    seq_blocks = seq2.reshape(count_b, width_q)
    blk_blocks = blk2.reshape(count_b, width_q)
    copy_blocks = copy2.reshape(count_b, width_q)

    def forward_block(item):
        q_block, q_seq, q_blk, q_copy = item
        scores = jnp.einsum("qhd,khd->hqk", q_block, keys, preferred_element_type=f32) * scale
        mask = allowed_pairs(q_seq, q_blk, q_copy, seq2, blk2, copy2)
        scores = jnp.where(mask[None], scores, -1e30)
        top = jnp.max(scores, axis=2, keepdims=True)
        lse = top + jnp.log(jnp.sum(jnp.exp(scores - top), axis=2, keepdims=True))
        probs = jnp.exp(scores - lse).astype(bf16)
        return (jnp.einsum("hqk,khd->qhd", probs, values, preferred_element_type=f32), lse[:, :, 0])

    attn_blocks, lse_blocks = lax.map(
        forward_block, (query_blocks, seq_blocks, blk_blocks, copy_blocks)
    )
    attn = attn_blocks.reshape(count, local_width).astype(bf16)
    attn_part = jnp.dot(attn, out_weight, preferred_element_type=f32).reshape(2, group_rows, width)
    attn_out = lax.psum_scatter(
        attn_part.astype(jnp.bfloat16), "narrow", scatter_dimension=1, tiled=True
    ).astype(jnp.float32)
    h_mid = resid + attn_out
    normed2, norm2_pull = jax.vjp(layer_norm, h_mid, ln2_gain, ln2_bias)
    b_all = lax.all_gather(normed2.astype(bf16), "narrow", axis=1, tiled=True).reshape(count, width)
    up_pre = jnp.dot(b_all, up_weight, preferred_element_type=f32) + up_bias
    hidden_f, gelu_pull = jax.vjp(gelu_tanh, up_pre)
    hidden = hidden_f.astype(bf16)
    down_part = jnp.dot(hidden, down_weight, preferred_element_type=f32).reshape(
        2, group_rows, width
    )
    mlp_out = lax.psum_scatter(
        down_part.astype(jnp.bfloat16), "narrow", scatter_dimension=1, tiled=True
    ).astype(jnp.float32)
    output = (h_mid + mlp_out + down_bias).astype(bf16)
    grad_out = cotangent.astype(f32)
    d_down_bias = jnp.sum(grad_out, axis=(0, 1))
    cot_all = lax.all_gather(cotangent, "narrow", axis=1, tiled=True).reshape(count, width)
    d_down = inner_rows(hidden, cot_all)
    d_hidden = times_trans(cot_all, down_weight)
    d_up_low = gelu_pull(d_hidden)[0].astype(bf16)
    d_up = inner_rows(b_all, d_up_low)
    d_up_bias = jnp.sum(d_up_low, axis=0, dtype=f32)
    d_b_part = times_trans(d_up_low, up_weight).reshape(2, group_rows, width)
    d_normed2 = lax.psum_scatter(
        d_b_part.astype(jnp.bfloat16), "narrow", scatter_dimension=1, tiled=True
    ).astype(jnp.float32)
    d_h_ln, d_ln2_gain, d_ln2_bias = norm2_pull(d_normed2)
    d_h_mid = grad_out + d_h_ln
    d_z = d_h_mid.astype(bf16)
    d_z_all = lax.all_gather(d_z, "narrow", axis=1, tiled=True).reshape(count, width)
    d_out = inner_rows(attn, d_z_all)
    d_attn = times_trans(d_z_all, out_weight).astype(bf16)
    d_attn_blocks = d_attn.reshape(count_b, width_q, heads_dev, HEAD)

    def backward_block(carry, item):
        d_keys, d_values = carry
        q_block, lse_block, d_block, q_seq, q_blk, q_copy = item
        scores = jnp.einsum("qhd,khd->hqk", q_block, keys, preferred_element_type=f32) * scale
        mask = allowed_pairs(q_seq, q_blk, q_copy, seq2, blk2, copy2)
        scores = jnp.where(mask[None], scores, -1e30)
        probs = jnp.exp(scores - lse_block[:, :, None])
        d_probs = jnp.einsum("qhd,khd->hqk", d_block, values, preferred_element_type=f32)
        delta = jnp.sum(d_probs * probs, axis=2, keepdims=True)
        d_scores = (probs * (d_probs - delta)).astype(bf16)
        d_query = jnp.einsum("hqk,khd->qhd", d_scores, keys, preferred_element_type=f32) * scale
        d_keys = (
            d_keys
            + jnp.einsum("hqk,qhd->khd", d_scores, q_block, preferred_element_type=f32) * scale
        )
        d_values = d_values + jnp.einsum(
            "hqk,qhd->khd", probs.astype(bf16), d_block, preferred_element_type=f32
        )
        return ((d_keys, d_values), d_query)

    empty = jnp.zeros((count, heads_dev, HEAD), f32)
    (d_keys, d_values), d_query_blocks = lax.scan(
        backward_block,
        (empty, empty),
        (query_blocks, lse_blocks, d_attn_blocks, seq_blocks, blk_blocks, copy_blocks),
    )
    d_q_low = (
        q_pull(d_query_blocks.reshape(count, heads_dev, HEAD))[0]
        .astype(bf16)
        .reshape(count, local_width)
    )
    d_k_low = k_pull(d_keys)[0].astype(bf16).reshape(count, local_width)
    d_v_low = d_values.astype(bf16).reshape(count, local_width)
    d_qkv = jnp.stack(
        [inner_rows(a_all, d_q_low), inner_rows(a_all, d_k_low), inner_rows(a_all, d_v_low)]
    )
    d_a_part = (
        times_trans(d_q_low, qkv_weight[0])
        + times_trans(d_k_low, qkv_weight[1])
        + times_trans(d_v_low, qkv_weight[2])
    ).reshape(2, group_rows, width)
    d_normed1 = lax.psum_scatter(
        d_a_part.astype(jnp.bfloat16), "narrow", scatter_dimension=1, tiled=True
    ).astype(jnp.float32)
    d_resid_ln, d_ln1_gain, d_ln1_bias = norm1_pull(d_normed1)
    d_resid = d_h_mid + d_resid_ln
    masked = noise[:, None] == 1
    d_tokens = (d_resid[1] + jnp.where(masked, 0.0, d_resid[0])).astype(bf16)
    d_mask = jnp.sum(jnp.where(masked, d_resid[0], 0.0), axis=0)
    summed = (
        lax.psum_scatter(d_qkv, "wide", scatter_dimension=1, tiled=True),
        lax.psum_scatter(d_out, "wide", scatter_dimension=1, tiled=True),
        lax.psum_scatter(d_up, "wide", scatter_dimension=0, tiled=True),
        lax.psum_scatter(d_down, "wide", scatter_dimension=1, tiled=True),
        lax.psum_scatter(d_up_bias[None, :], "wide", scatter_dimension=1, tiled=True),
    )
    small = lax.psum(
        (d_ln1_gain, d_ln1_bias, d_ln2_gain, d_ln2_bias, d_down_bias, d_mask), ("wide", "narrow")
    )
    return (
        output,
        d_tokens,
        small[0],
        small[1],
        summed[0],
        summed[1],
        small[2],
        small[3],
        summed[2],
        summed[4][0],
        summed[3],
        small[4],
        small[5],
    )


def solution(mesh):
    placed = (
        P(("wide", "narrow"), None),
        P(("wide", "narrow")),
        P("wide", None),
        P(),
        P(),
        P(None, None, "narrow"),
        P("narrow", None),
        P(),
        P(),
        P(None, "narrow"),
        P("narrow"),
        P("narrow", None),
        P(),
        P(),
        P(None, ("wide", "narrow"), None),
    )
    return jax.shard_map(
        per_device,
        mesh=mesh,
        in_specs=placed,
        out_specs=(
            P(None, ("wide", "narrow"), None),
            P(("wide", "narrow"), None),
            P(),
            P(),
            P(None, "wide", "narrow"),
            P("narrow", "wide"),
            P(),
            P(),
            P("wide", "narrow"),
            P(("narrow", "wide")),
            P("narrow", "wide"),
            P(),
            P(),
        ),
        check_vma=False,
    )
```

profile of v0, /device:TPU:0, one launch (start us, length us, event | category | flops | bytes accessed | tf_op | source)
XLA Modules:
  0.0 2366.9 jit_solution(2762413686105143079)
XLA Ops:
  20.2 113.0 %all-gather.5.cloned.1.call-done = bf16[2,2048,768]{2,1,0:T(8,128)(2,1)} async-done(((bf16[2,512,768]{2,1,0:T(8,128)(2,1)}), bf16[2,2048,768]{2,1,0:T(8,128)(2,1)}) %all-gather.5.cloned.1.call-update) | async-done | bytes 6291472 | tf_op jit(solution)/shard_map/all_gather | solution.py:104
  148.6 346.6 %while.27 = (s32[]{:T(128)}, bf16[8,512,3,64]{1,3,2,0:T(8,128)(2,1)}, f32[8,3,512]{2,1,0:T(4,128)}, s32[8,512]{1,0:T(8,128)}, s32[4096]{0:T(1024)S(1)}, /*index=...) while((s32[]{:T(128)}, ...), condition=%wide.region_8.9_spmd, body=%wide.region_5.8_spmd.sunk | while | flops 1696594944 | bytes 94020792 | solution.py:147
  167.1 11.9 exponential_reduce_fusion.2
  179.6 12.3 fusion.154
  198.7 11.7 fusion.153
  210.4 11.9 exponential_reduce_fusion.2
  223.0 12.3 fusion.154
  242.1 11.7 fusion.153
  253.7 11.9 exponential_reduce_fusion.2
  266.3 12.3 fusion.154
  297.1 11.9 exponential_reduce_fusion.2
  309.6 12.3 fusion.154
  340.4 11.9 exponential_reduce_fusion.2
  352.9 12.3 fusion.154
  383.7 11.9 exponential_reduce_fusion.2
  396.3 12.3 fusion.154
  427.0 11.9 exponential_reduce_fusion.2
  439.6 12.3 fusion.154
  470.4 11.9 exponential_reduce_fusion.2
  482.9 12.3 fusion.154
  508.9 109.1 %reduce-scatter.16.cloned.1.call-done = bf16[2,512,768]{2,1,0:T(8,128)(2,1)} async-done(((bf16[2,2048,768]{2,1,0:T(8,128)(2,1)}), bf16[2,512,768]{2,1,0:T(8,128)(2,1)}) %reduce-scatter.16.cloned.1.call-update) | async-done | bytes 1572880 | tf_op jit(solution)/shard_map/reduce_scatter | solution.py:152
  624.9 115.4 %all-gather.7.cloned.1.call-done = bf16[2,2048,768]{2,1,0:T(8,128)(2,1)} async-done(((bf16[2,512,768]{2,1,0:T(8,128)(2,1)}), bf16[2,2048,768]{2,1,0:T(8,128)(2,1)}) %all-gather.7.cloned.1.call-update) | async-done | bytes 6291472 | tf_op jit(solution)/shard_map/all_gather | solution.py:157
  750.8 104.4 %all-gather.9.cloned.1.call-done = bf16[2,2048,768]{2,1,0:T(8,128)(2,1)} async-done(((bf16[2,512,768]{2,1,0:T(8,128)(2,1)}), bf16[2,2048,768]{2,1,0:T(8,128)(2,1)}) %all-gather.9.cloned.1.call-update) | async-done | bytes 6291472 | tf_op jit(solution)/shard_map/all_gather | solution.py:170
  855.2 18.5 convert_reduce_fusion
  880.8 109.1 %reduce-scatter.20.cloned.1.call-done = bf16[2,512,768]{2,1,0:T(8,128)(2,1)} async-done(((bf16[2,2048,768]{2,1,0:T(8,128)(2,1)}), bf16[2,512,768]{2,1,0:T(8,128)(2,1)}) %reduce-scatter.20.cloned.1.call-update) | async-done | bytes 1572880 | tf_op jit(solution)/shard_map/reduce_scatter | solution.py:177
  1003.5 111.3 %all-gather.11.cloned.1.call-done = bf16[2,2048,768]{2,1,0:T(8,128)(2,1)} async-done(((bf16[2,512,768]{2,1,0:T(8,128)(2,1)}), bf16[2,2048,768]{2,1,0:T(8,128)(2,1)}) %all-gather.11.cloned.1.call-update) | async-done | bytes 6291472 | tf_op jit(solution)/shard_map/all_gather | solution.py:183
  1128.3 818.9 %while.28 = (s32[]{:T(128)}, f32[4096,3,64]{0,2,1:T(8,128)}, f32[4096,3,64]{0,2,1:T(8,128)}, f32[8,512,3,64]{1,0,3,2:T(8,128)}, bf16[8,512,3,64]{1,3,2,0:T(8,128...) while((s32[]{:T(128)}, f32[4096,3,64]{0,2,1:T(8,128)}, ...), condition=%wide.region_18.19_spmd.clone, body=%wide.region_16.18_spmd.clone.sunk | while | flops 4141710336 | bytes 229868800 | solution.py:209
  1136.0 13.3 fusion.164
  1149.4 13.0 fusion.166
  1162.4 18.2 multiply_reduce_fusion.4
  1180.6 21.7 multiply_convert_fusion.3
  1236.8 13.3 fusion.164
  1250.1 13.8 fusion.166
  1264.0 18.2 multiply_reduce_fusion.4
  1282.2 21.7 multiply_convert_fusion.3
  1339.3 13.3 fusion.164
  1352.6 13.8 fusion.166
  1366.4 18.2 multiply_reduce_fusion.4
  1384.6 21.7 multiply_convert_fusion.3
  1441.8 13.3 fusion.164
  1455.1 13.8 fusion.166
  1468.9 18.2 multiply_reduce_fusion.4
  1487.1 21.7 multiply_convert_fusion.3
  1544.3 13.3 fusion.164
  1557.6 13.8 fusion.166
  1571.4 18.2 multiply_reduce_fusion.4
  1589.6 21.7 multiply_convert_fusion.3
  1646.8 13.3 fusion.164
  1660.1 13.8 fusion.166
  1673.9 18.2 multiply_reduce_fusion.4
  1692.1 21.7 multiply_convert_fusion.3
  1749.3 13.3 fusion.164
  1762.6 13.8 fusion.166
  1776.4 18.2 multiply_reduce_fusion.4
  1794.6 21.7 multiply_convert_fusion.3
  1851.8 13.3 fusion.164
  1865.1 13.8 fusion.166
  1878.9 18.2 multiply_reduce_fusion.4
  1897.1 21.7 multiply_convert_fusion.3
  2001.0 13.5 add_convert_fusion
  2050.2 103.0 %reduce-scatter.22.cloned.1.call-done = bf16[2,512,768]{2,1,0:T(8,128)(2,1)} async-done(((bf16[2,2048,768]{2,1,0:T(8,128)(2,1)}), bf16[2,512,768]{2,1,0:T(8,128)(2,1)}) %reduce-scatter.22.cloned.1.call-update) | async-done | bytes 1572880 | tf_op jit(solution)/shard_map/reduce_scatter | solution.py:229
  2158.3 108.6 %reduce-scatter.18.cloned.1.call-done = bf16[2,512,768]{2,1,0:T(8,128)(2,1)} async-done(((bf16[2,2048,768]{2,1,0:T(8,128)(2,1)}), bf16[2,512,768]{2,1,0:T(8,128)(2,1)}) %reduce-scatter.18.cloned.1.call-update) | async-done | bytes 1572880 | tf_op jit(solution)/shard_map/reduce_scatter | solution.py:164
  2275.0 41.5 %all-reduce.4 = (f32[768]{0:T(1024)}, f32[768]{0:T(1024)}, f32[768]{0:T(1024)}, f32[768]{0:T(1024)}, f32[768]{0:T(1024)}, /*index=5*/f32[768]{0:T(1024)}) all-reduce(f32[768]{0:T(1024)S(1)} %get-tuple-element.328, f32[768]{0:T(1024)S(1)} %get-tuple-element.332, ...), channel_id=1, replica_groups=mesh['wide'=8,'narrow'=4] {'wide','narrow'}, use_global_device_ids=true, to_apply=%region_23.24 | all-reduce | flops 4608 | bytes 36864 | tf_op jit(solution)/shard_map/psum | solution.py:244
  2316.5 43.7 %reduce-scatter.26.cloned.1.call-done = f32[768,96]{0,1:T(8,128)} async-done(((f32[768,768]{0,1:T(8,128)}), f32[768,96]{0,1:T(8,128)}) %reduce-scatter.26.cloned.1.call-update) | async-done | bytes 294928 | tf_op jit(solution)/shard_map/reduce_scatter | solution.py:241
  (377 shorter events, 607.4 us)
Async XLA Ops:
  7.2 848.0 %copy-start = (bf16[768,768]{1,0:T(8,128)(2,1)S(1)}, bf16[768,768]{1,0:T(8,128)(2,1)}, u32[]{:S(2)}) copy-start(bf16[768,768]{1,0:T(8,128)(2,1)} %param.30) | copy-start | bytes 3538948
  7.2 126.0 %all-gather.5.cloned.1.call-start = ((), (), s32[]{:S(2)}) async-start(), calls=%async_computation.9 | async-start | bytes 7864320 | tf_op jit(solution)/shard_map/all_gather | solution.py:104
  9.3 3.3 copy-start.6
  13.2 3.5 copy-start.23
  15.0 603.0 %reduce-scatter.16.cloned.1.call-start = ((), (), s32[]{:S(2)}) async-start(), calls=%async_computation.10 | async-start | bytes 7864320 | tf_op jit(solution)/shard_map/reduce_scatter | solution.py:152
  133.2 6.3 copy-start.52
  167.1 12.6 copy-start.10
  210.4 12.6 copy-start.10
  253.7 12.6 copy-start.10
  297.1 12.6 copy-start.10
  340.4 12.6 copy-start.10
  383.7 12.6 copy-start.10
  427.0 12.6 copy-start.10
  470.4 12.6 copy-start.10
  495.2 7.1 copy-start.26
  508.8 231.4 %all-gather.7.cloned.1.call-start = ((), (), s32[]{:S(2)}) async-start(), calls=%async_computation.11 | async-start | bytes 7864320 | tf_op jit(solution)/shard_map/all_gather | solution.py:157
  620.7 375.8 %copy-start.27 = (f32[2,512]{1,0:T(2,128)}, f32[2,512]{1,0:T(2,128)S(1)}, u32[]{:S(2)}) copy-start(f32[2,512]{1,0:T(2,128)S(1)} %broadcast_multiply_fusion.2) | copy-start | bytes 12292
  622.5 374.0 %copy-start.33 = (f32[2,512]{1,0:T(2,128)}, f32[2,512]{1,0:T(2,128)S(1)}, u32[]{:S(2)}) copy-start(f32[2,512]{1,0:T(2,128)S(1)} %fusion.81) | copy-start | bytes 12292
  624.2 231.0 %all-gather.9.cloned.1.call-start = ((), (), s32[]{:S(2)}) async-start(), calls=%async_computation.13 | async-start | bytes 7864320 | tf_op jit(solution)/shard_map/all_gather | solution.py:170
  624.8 365.1 %reduce-scatter.20.cloned.1.call-start = ((), (), s32[]{:S(2)}) async-start(), calls=%async_computation.14 | async-start | bytes 7864320 | tf_op jit(solution)/shard_map/reduce_scatter | solution.py:177
  740.2 115.0 %copy-start.55 = (f32[768]{0:T(1024)S(1)}, f32[768]{0:T(1024)}, u32[]{:S(2)}) copy-start(f32[768]{0:T(1024)} %param.29) | copy-start | bytes 9220
  855.2 18.5 copy-start.54
  873.7 7.0 copy-start.57
  880.8 234.0 %all-gather.11.cloned.1.call-start = ((), (), s32[]{:S(2)}) async-start(), calls=%async_computation.15 | async-start | bytes 7864320 | tf_op jit(solution)/shard_map/all_gather | solution.py:183
  989.9 4.2 copy-start.5
  989.9 4.2 copy-start.11
  994.1 4.6 copy-start.35
  998.8 1046.3 %reduce-scatter.32.cloned.1.call-start = ((), (), s32[]{:S(2)}) async-start(), calls=%async_computation.21 | async-start | bytes 442368
  1003.4 1043.1 %reduce-scatter.30.cloned.1.call-start = ((), (), s32[]{:S(2)}) async-start(), calls=%async_computation.20 | async-start | bytes 884736
  1114.8 6.3 copy-start.25
  1114.8 6.3 copy-start.53
  1211.2 18.1 copy-start.3
  1312.8 19.0 copy-start.3
  1415.3 19.0 copy-start.3
  1517.8 19.0 copy-start.3
  1620.3 19.0 copy-start.3
  1722.8 19.0 copy-start.3
  1825.3 19.0 copy-start.3
  1927.8 19.0 copy-start.3
  1951.8 10.2 slice-start
  1954.1 7.9 copy-start.21
  1954.9 7.0 slice-start.1
  1963.4 84.8 %reduce-scatter.28.cloned.1.call-start = ((), (), s32[]{:S(2)}) async-start(), calls=%async_computation.19 | async-start | bytes 2211840
  1969.0 5.5 copy-start.18
  1969.0 5.5 copy-start.20
  1986.4 8.2 copy-start.19
  1986.4 166.9 %reduce-scatter.22.cloned.1.call-start = ((), (), s32[]{:S(2)}) async-start(), calls=%async_computation.16 | async-start | bytes 7864320 | tf_op jit(solution)/shard_map/reduce_scatter | solution.py:229
  1986.6 8.0 copy-start.24
  1994.6 6.4 copy-start.22
  2014.6 252.3 %reduce-scatter.18.cloned.1.call-start = ((), (), s32[]{:S(2)}) async-start(), calls=%async_computation.12 | async-start | bytes 7864320 | tf_op jit(solution)/shard_map/reduce_scatter | solution.py:164
  2024.3 292.1 %reduce-scatter.24.cloned.1.call-start = ((), (), s32[]{:S(2)}) async-start(), calls=%async_computation.17 | async-start | bytes 2654208 | tf_op jit(solution)/shard_map/reduce_scatter | solution.py:240
  2034.6 325.5 %reduce-scatter.26.cloned.1.call-start = ((), (), s32[]{:S(2)}) async-start(), calls=%async_computation.18 | async-start | bytes 2654208 | tf_op jit(solution)/shard_map/reduce_scatter | solution.py:241
  2045.0 108.3 %copy-start.7 = (f32[1,512,768]{2,1,0:T(8,128)S(1)}, f32[1,512,768]{2,1,0:T(8,128)}, u32[]{:S(2)}) copy-start(f32[1,512,768]{2,1,0:T(8,128)} %copy-done.6) | copy-start | bytes 4718596
  2045.0 108.3 %copy-start.30 = (f32[2,512]{1,0:T(2,128)S(1)}, f32[2,512]{1,0:T(2,128)}, u32[]{:S(2)}) copy-start(f32[2,512]{1,0:T(2,128)} %copy-done.29) | copy-start | bytes 12292
  2045.0 108.3 %copy-start.38 = (f32[768]{0:T(1024)S(1)}, f32[768]{0:T(1024)}, u32[]{:S(2)}) copy-start(f32[768]{0:T(1024)} %param.22) | copy-start | bytes 9220
  2045.1 111.4 %copy-start.44 = (f32[2,512]{1,0:T(2,128)S(1)}, f32[2,512]{1,0:T(2,128)}, u32[]{:S(2)}) copy-start(f32[2,512]{1,0:T(2,128)} %copy-done.43) | copy-start | bytes 12292
  2046.6 109.9 %copy-start.40 = (f32[2,512]{1,0:T(2,128)S(1)}, f32[2,512]{1,0:T(2,128)}, u32[]{:S(2)}) copy-start(f32[2,512]{1,0:T(2,128)} %copy-done.39) | copy-start | bytes 12292
  2156.4 110.5 %copy-start.28 = (f32[2,512]{1,0:T(2,128)S(1)}, f32[2,512]{1,0:T(2,128)}, u32[]{:S(2)}) copy-start(f32[2,512]{1,0:T(2,128)} %copy-done.27) | copy-start | bytes 12292
  2156.4 110.5 %copy-start.32 = (f32[768]{0:T(1024)S(1)}, f32[768]{0:T(1024)}, u32[]{:S(2)}) copy-start(f32[768]{0:T(1024)} %param.26) | copy-start | bytes 9220
  2156.4 110.5 %copy-start.34 = (f32[2,512]{1,0:T(2,128)S(1)}, f32[2,512]{1,0:T(2,128)}, u32[]{:S(2)}) copy-start(f32[2,512]{1,0:T(2,128)} %copy-done.33) | copy-start | bytes 12292
  2156.4 110.5 %copy-start.36 = (f32[2,512]{1,0:T(2,128)S(1)}, f32[2,512]{1,0:T(2,128)}, u32[]{:S(2)}) copy-start(f32[2,512]{1,0:T(2,128)} %copy-done.35) | copy-start | bytes 12292
  2156.4 110.5 %copy-start.42 = (f32[2,512]{1,0:T(2,128)S(1)}, f32[2,512]{1,0:T(2,128)}, u32[]{:S(2)}) copy-start(f32[2,512]{1,0:T(2,128)} %copy-done.41) | copy-start | bytes 12292
  2156.5 110.5 %copy-start.51 = (f32[768]{0:T(1024)S(1)}, f32[768]{0:T(1024)}, u32[]{:S(2)}) copy-start(f32[768]{0:T(1024)} %param.31) | copy-start | bytes 9220
  2158.3 115.5 %copy-start.48 = (pred[512]{0:T(512)(128)(4,1)S(1)}, pred[512]{0:T(512)(128)(4,1)}, u32[]{:S(2)}) copy-start(pred[512]{0:T(512)(128)(4,1)} %copy-done.47) | copy-start | bytes 1540
  (30 other events, 52.0 us)
Sparse Core Ops, SparseCore 0:
  15.1 118.0 all-gather.4
  509.0 108.9 reduce-scatter.15
  624.4 115.8 all-gather.6
  741.7 113.5 all-gather.8
  880.9 108.9 reduce-scatter.19
  998.9 115.8 all-gather.10
  1117.8 32.0 reduce-scatter.31
  1963.5 33.0 reduce-scatter.29
  2000.1 40.1 reduce-scatter.27
  2042.5 110.7 reduce-scatter.21
  2155.6 111.2 reduce-scatter.17
  2270.7 42.9 reduce-scatter.23
  2317.6 42.4 reduce-scatter.25
where the time goes:
time: 2380 us; the launch traced here: 2370 us
  waiting for transfers between devices  918 us (39%)
  matrix products  833 us (35%)
  other arithmetic  427 us (18%)
  local copies, waits for them, and re-layouts  130 us (5%)
  blocking collectives  41.5 us (2%)
    convert_element_type x8, other arithmetic, backward_block(): d_scores = (probs * (d_probs - delta)).astype(bf16)  174 us
    dot_general x8, matrix products, backward_block(): jnp.einsum('qhd,khd->hqk', d_block, values, preferred_element_type=f32)  146 us
    all_gather x1, waiting for transfers between devices, per_device(): lax.all_gather(normed2.astype(bf16), 'narrow', axis=1, tiled=True)  115 us
    all_gather x1, waiting for transfers between devices, per_device(): lax.all_gather(normed1.astype(bf16), 'narrow', axis=1, tiled=True)  113 us
    all_gather x1, waiting for transfers between devices, per_device(): lax.all_gather(d_z, 'narrow', axis=1, tiled=True).reshape(count, width)  111 us
    dot_general x8, matrix products, backward_block(): jnp.einsum('hqk,qhd->khd', probs.astype(bf16), d_block, preferred_element...  110 us
    reduce_scatter x1, waiting for transfers between devices, per_device(): lax.psum_scatter(attn_part.astype(jnp.bfloat16), 'narrow', scatter_dimens...  109 us
    reduce_scatter x1, waiting for transfers between devices, per_device(): lax.psum_scatter(d_b_part.astype(jnp.bfloat16), 'narrow', scatter_dimensi...  109 us
  transfers between devices with their start and end apart: 13, of which 9 were waited for; matrix products, arithmetic and copies ran while one was open for 41% of the time, Pallas kernels for 0%

commit v1 on v0

--- a/solution.py
+++ b/solution.py
@@ -7,6 +7,27 @@
 HEAD = 64
 BLOCK = 16
 EPS = 1e-05
+
+
+def ring_gather(shard, axis, dim):
+    peers, index, rows = (lax.axis_size(axis), lax.axis_index(axis), shard.shape[dim])
+    ahead = [(i, (i + 1) % peers) for i in range(peers)]
+    downward = [(i, (i - 1) % peers) for i in range(peers)]
+    result = jnp.zeros((*shard.shape[:dim], peers * rows, *shard.shape[dim + 1 :]), shard.dtype)
+    result = lax.dynamic_update_slice_in_dim(result, shard, index * rows, axis=dim)
+    from_left = from_right = shard
+    middle = peers // 2
+    for step in range(1, middle + 1):
+        from_left = lax.ppermute(from_left, axis, ahead)
+        result = lax.dynamic_update_slice_in_dim(
+            result, from_left, (index - step) % peers * rows, axis=dim
+        )
+        if step < peers - middle:
+            from_right = lax.ppermute(from_right, axis, downward)
+            result = lax.dynamic_update_slice_in_dim(
+                result, from_right, (index + step) % peers * rows, axis=dim
+            )
+    return result
 
 
 def layer_norm(values, gain, shift):
@@ -167,7 +188,7 @@
     output = (h_mid + mlp_out + down_bias).astype(bf16)
     grad_out = cotangent.astype(f32)
     d_down_bias = jnp.sum(grad_out, axis=(0, 1))
-    cot_all = lax.all_gather(cotangent, "narrow", axis=1, tiled=True).reshape(count, width)
+    cot_all = ring_gather(cotangent, "narrow", 1).reshape(count, width)
     d_down = inner_rows(hidden, cot_all)
     d_hidden = times_trans(cot_all, down_weight)
     d_up_low = gelu_pull(d_hidden)[0].astype(bf16)

time: 2380 us -> 2370 us (level)
  waiting for transfers between devices: 918 us -> 832 us
  starting transfers between devices: 1.39 us -> 65.2 us
    ppermute x0 -> x3, waiting for transfers between devices: none -> 125 us  [the longest x2 109 us: ring_gather(): from_left = lax.ppermute(from_left, axis, ahead)]
    all_gather x1, waiting for transfers between devices: 115 us -> 5.84 us  [per_device(): lax.all_gather(normed2.astype(bf16), 'narrow', axis=1, tiled=True)]
    all_gather x1 -> x0, waiting for transfers between devices: 104 us -> none  [per_device(): lax.all_gather(cotangent, 'narrow', axis=1, tiled=True)]
    ppermute x0 -> x3, starting transfers between devices: none -> 63.9 us  [the longest x2 61.6 us: ring_gather(): from_left = lax.ppermute(from_left, axis, ahead)]
  transfers between devices with their start and end apart: 13 -> 15, of which waited for: 9 -> 11; matrix products, arithmetic and copies ran while one was open for 41% -> 41% of each run, Pallas kernels for 0% -> 0%
where the time goes in v1:
time: 2370 us; the launch traced here: 2360 us
  matrix products  834 us (35%)
  waiting for transfers between devices  832 us (35%)
  other arithmetic  427 us (18%)
  local copies, waits for them, and re-layouts  142 us (6%)
  starting transfers between devices  65.2 us (3%)
  blocking collectives  41.4 us (2%)
    convert_element_type x8, other arithmetic, backward_block(): d_scores = (probs * (d_probs - delta)).astype(bf16)  174 us
    dot_general x8, matrix products, backward_block(): jnp.einsum('qhd,khd->hqk', d_block, values, preferred_element_type=f32)  146 us
    all_gather x1, waiting for transfers between devices, per_device(): lax.all_gather(normed1.astype(bf16), 'narrow', axis=1, tiled=True)  113 us
    reduce_scatter x1, waiting for transfers between devices, per_device(): lax.psum_scatter(d_b_part.astype(jnp.bfloat16), 'narrow', scatter_dimensi...  112 us
    all_gather x1, waiting for transfers between devices, per_device(): lax.all_gather(d_z, 'narrow', axis=1, tiled=True).reshape(count, width)  111 us
    dot_general x8, matrix products, backward_block(): jnp.einsum('hqk,qhd->khd', probs.astype(bf16), d_block, preferred_element...  111 us
    ppermute x2, waiting for transfers between devices, ring_gather(): from_left = lax.ppermute(from_left, axis, ahead)  109 us
    reduce_scatter x1, waiting for transfers between devices, per_device(): lax.psum_scatter(attn_part.astype(jnp.bfloat16), 'narrow', scatter_dimens...  109 us
  transfers between devices with their start and end apart: 15, of which 11 were waited for; matrix products, arithmetic and copies ran while one was open for 41% of the time, Pallas kernels for 0%

profile of v1, /device:TPU:0, one launch (start us, length us, event | category | flops | bytes accessed | tf_op | source)
XLA Modules:
  0.0 2358.4 jit_solution(6969092854187254237)
XLA Ops:
  20.2 113.0 %all-gather.4.cloned.1.call-done = bf16[2,2048,768]{2,1,0:T(8,128)(2,1)} async-done(((bf16[2,512,768]{2,1,0:T(8,128)(2,1)}), bf16[2,2048,768]{2,1,0:T(8,128)(2,1)}) %all-gather.4.cloned.1.call-update) | async-done | bytes 6291472 | tf_op jit(solution)/shard_map/all_gather | solution.py:125
  148.6 347.0 %while.27 = (s32[]{:T(128)}, bf16[8,512,3,64]{1,3,2,0:T(8,128)(2,1)}, f32[8,3,512]{2,1,0:T(4,128)}, s32[8,512]{1,0:T(8,128)}, s32[4096]{0:T(1024)S(1)}, /*index=...) while((s32[]{:T(128)}, ...), condition=%wide.region_8.9_spmd, body=%wide.region_5.8_spmd.sunk | while | flops 1696594944 | bytes 94020792 | solution.py:168
  167.2 11.9 exponential_reduce_fusion.2
  179.7 12.3 fusion.154
  210.5 11.9 exponential_reduce_fusion.2
  223.1 12.3 fusion.154
  253.9 11.9 exponential_reduce_fusion.2
  266.5 12.3 fusion.154
  297.3 11.9 exponential_reduce_fusion.2
  309.8 12.3 fusion.154
  340.7 11.9 exponential_reduce_fusion.2
  353.2 12.3 fusion.154
  384.0 11.9 exponential_reduce_fusion.2
  396.6 12.3 fusion.154
  427.4 11.9 exponential_reduce_fusion.2
  440.0 12.3 fusion.154
  470.8 11.9 exponential_reduce_fusion.2
  483.3 12.3 fusion.154
  509.3 109.1 %reduce-scatter.16.cloned.1.call-done = bf16[2,512,768]{2,1,0:T(8,128)(2,1)} async-done(((bf16[2,2048,768]{2,1,0:T(8,128)(2,1)}), bf16[2,512,768]{2,1,0:T(8,128)(2,1)}) %reduce-scatter.16.cloned.1.call-update) | async-done | bytes 1572880 | tf_op jit(solution)/shard_map/reduce_scatter | solution.py:173
  628.6 60.9 %collective-permute-done = bf16[2,512,768]{2,1,0:T(8,128)(2,1)} collective-permute-done((bf16[2,512,768]{2,1,0:T(8,128)(2,1)}, bf16[2,512,768]{2,1,0:T(8,128)(2,1)}, u32[]{:S(2)}, u32[]{:S(2)}) %collective-permute-start) | collective-permute-done | bytes 1572896 | tf_op jit(solution)/shard_map/ppermute | solution.py:21
  689.5 60.0 %collective-permute-start.2 = (bf16[2,512,768]{2,1,0:T(8,128)(2,1)}, bf16[2,512,768]{2,1,0:T(8,128)(2,1)}, u32[]{:S(2)}, u32[]{:S(2)}) collective-permute-start(bf16[2,512,768]{2,1,0:T(8,128)(2,1)} %collective-permute-done), channel_id=1, source_target_pairs={{0,1},{1,2},{2,3},{3,0},{4,5},{5,6},{6,7},{7,4},{8,9},{9,10},{10,1... | collective-permute-start | bytes 4718600 | tf_op jit(solution)/shard_map/ppermute | solution.py:21
  756.5 15.6 collective-permute-done.1
  774.9 48.3 %collective-permute-done.2 = bf16[2,512,768]{2,1,0:T(8,128)(2,1)} collective-permute-done((bf16[2,512,768]{2,1,0:T(8,128)(2,1)}, bf16[2,512,768]{2,1,0:T(8,128)(2,1)}, u32[]{:S(2)}, u32[]{:S(2)}) %collective-permute-start.2) | collective-permute-done | bytes 1572896 | tf_op jit(solution)/shard_map/ppermute | solution.py:21
  842.0 18.4 convert_reduce_fusion
  867.6 112.1 %reduce-scatter.20.cloned.1.call-done = bf16[2,512,768]{2,1,0:T(8,128)(2,1)} async-done(((bf16[2,2048,768]{2,1,0:T(8,128)(2,1)}), bf16[2,512,768]{2,1,0:T(8,128)(2,1)}) %reduce-scatter.20.cloned.1.call-update) | async-done | bytes 1572880 | tf_op jit(solution)/shard_map/reduce_scatter | solution.py:198
  993.2 111.3 %all-gather.8.cloned.1.call-done = bf16[2,2048,768]{2,1,0:T(8,128)(2,1)} async-done(((bf16[2,512,768]{2,1,0:T(8,128)(2,1)}), bf16[2,2048,768]{2,1,0:T(8,128)(2,1)}) %all-gather.8.cloned.1.call-update) | async-done | bytes 6291472 | tf_op jit(solution)/shard_map/all_gather | solution.py:204
  1118.0 820.2 %while.28 = (s32[]{:T(128)}, f32[4096,3,64]{0,2,1:T(8,128)}, f32[4096,3,64]{0,2,1:T(8,128)}, f32[8,512,3,64]{1,0,3,2:T(8,128)}, bf16[8,512,3,64]{1,3,2,0:T(8,128...) while((s32[]{:T(128)}, f32[4096,3,64]{0,2,1:T(8,128)}, ...), condition=%wide.region_18.19_spmd.clone, body=%wide.region_16.18_spmd.clone.sunk | while | flops 4141710336 | bytes 229868800 | solution.py:230
  1125.8 13.4 fusion.164
  1139.1 13.1 fusion.166
  1152.2 18.2 multiply_reduce_fusion.4
  1170.4 21.8 multiply_convert_fusion.3
  1226.7 13.3 fusion.164
  1240.0 13.9 fusion.166
  1254.0 18.2 multiply_reduce_fusion.4
  1272.2 21.8 multiply_convert_fusion.3
  1329.4 13.3 fusion.164
  1342.7 13.9 fusion.166
  1356.6 18.2 multiply_reduce_fusion.4
  1374.8 21.8 multiply_convert_fusion.3
  1432.0 13.3 fusion.164
  1445.3 13.9 fusion.166
  1459.3 18.2 multiply_reduce_fusion.4
  1477.5 21.8 multiply_convert_fusion.3
  1534.7 13.3 fusion.164
  1548.0 13.9 fusion.166
  1561.9 18.2 multiply_reduce_fusion.4
  1580.1 21.8 multiply_convert_fusion.3
  1637.3 13.3 fusion.164
  1650.6 13.9 fusion.166
  1664.6 18.2 multiply_reduce_fusion.4
  1682.8 21.8 multiply_convert_fusion.3
  1740.0 13.3 fusion.164
  1753.3 13.9 fusion.166
  1767.2 18.2 multiply_reduce_fusion.4
  1785.4 21.8 multiply_convert_fusion.3
  1842.6 13.3 fusion.164
  1855.9 13.9 fusion.166
  1869.9 18.3 multiply_reduce_fusion.4
  1888.1 21.8 multiply_convert_fusion.3
  1992.0 13.5 add_convert_fusion
  2041.1 103.4 %reduce-scatter.22.cloned.1.call-done = bf16[2,512,768]{2,1,0:T(8,128)(2,1)} async-done(((bf16[2,2048,768]{2,1,0:T(8,128)(2,1)}), bf16[2,512,768]{2,1,0:T(8,128)(2,1)}) %reduce-scatter.22.cloned.1.call-update) | async-done | bytes 1572880 | tf_op jit(solution)/shard_map/reduce_scatter | solution.py:250
  2149.6 108.4 %reduce-scatter.18.cloned.1.call-done = bf16[2,512,768]{2,1,0:T(8,128)(2,1)} async-done(((bf16[2,2048,768]{2,1,0:T(8,128)(2,1)}), bf16[2,512,768]{2,1,0:T(8,128)(2,1)}) %reduce-scatter.18.cloned.1.call-update) | async-done | bytes 1572880 | tf_op jit(solution)/shard_map/reduce_scatter | solution.py:185
  2266.1 41.4 %all-reduce.4 = (f32[768]{0:T(1024)}, f32[768]{0:T(1024)}, f32[768]{0:T(1024)}, f32[768]{0:T(1024)}, f32[768]{0:T(1024)}, /*index=5*/f32[768]{0:T(1024)}) all-reduce(f32[768]{0:T(1024)S(1)} %get-tuple-element.328, f32[768]{0:T(1024)S(1)} %get-tuple-element.332, ...), channel_id=1, replica_groups=mesh['wide'=8,'narrow'=4] {'wide','narrow'}, use_global_device_ids=true, to_apply=%region_23.24 | all-reduce | flops 4608 | bytes 36864 | tf_op jit(solution)/shard_map/psum | solution.py:265
  2307.5 43.8 %reduce-scatter.26.cloned.1.call-done = f32[768,96]{0,1:T(8,128)} async-done(((f32[768,768]{0,1:T(8,128)}), f32[768,96]{0,1:T(8,128)}) %reduce-scatter.26.cloned.1.call-update) | async-done | bytes 294928 | tf_op jit(solution)/shard_map/reduce_scatter | solution.py:262
  (387 shorter events, 652.4 us)
Async XLA Ops:
  7.2 834.8 %copy-start = (bf16[768,768]{1,0:T(8,128)(2,1)S(1)}, bf16[768,768]{1,0:T(8,128)(2,1)}, u32[]{:S(2)}) copy-start(bf16[768,768]{1,0:T(8,128)(2,1)} %param.30) | copy-start | bytes 3538948
  7.2 126.0 %all-gather.4.cloned.1.call-start = ((), (), s32[]{:S(2)}) async-start(), calls=%async_computation.9 | async-start | bytes 7864320 | tf_op jit(solution)/shard_map/all_gather | solution.py:125
  15.0 603.4 %reduce-scatter.16.cloned.1.call-start = ((), (), s32[]{:S(2)}) async-start(), calls=%async_computation.10 | async-start | bytes 7864320 | tf_op jit(solution)/shard_map/reduce_scatter | solution.py:173
  133.2 6.3 copy-start.53
  167.2 12.6 copy-start.10
  210.5 12.6 copy-start.10
  253.9 12.6 copy-start.10
  297.3 12.6 copy-start.10
  340.7 12.6 copy-start.10
  384.0 12.6 copy-start.10
  427.4 12.6 copy-start.10
  470.8 12.6 copy-start.10
  495.6 7.1 copy-start.27
  509.3 322.5 %all-gather.6.cloned.1.call-start = ((), (), s32[]{:S(2)}) async-start(), calls=%async_computation.11 | async-start | bytes 7864320 | tf_op jit(solution)/shard_map/all_gather | solution.py:178
  621.2 365.1 %copy-start.28 = (f32[2,512]{1,0:T(2,128)}, f32[2,512]{1,0:T(2,128)S(1)}, u32[]{:S(2)}) copy-start(f32[2,512]{1,0:T(2,128)S(1)} %broadcast_multiply_fusion.2) | copy-start | bytes 12292
  622.9 363.3 %copy-start.34 = (f32[2,512]{1,0:T(2,128)}, f32[2,512]{1,0:T(2,128)S(1)}, u32[]{:S(2)}) copy-start(f32[2,512]{1,0:T(2,128)S(1)} %fusion.81) | copy-start | bytes 12292
  624.7 355.0 %reduce-scatter.20.cloned.1.call-start = ((), (), s32[]{:S(2)}) async-start(), calls=%async_computation.13 | async-start | bytes 7864320 | tf_op jit(solution)/shard_map/reduce_scatter | solution.py:198
  624.7 64.8 %collective-permute-start = (bf16[2,512,768]{2,1,0:T(8,128)(2,1)}, bf16[2,512,768]{2,1,0:T(8,128)(2,1)}, u32[]{:S(2)}, u32[]{:S(2)}) collective-permute-start(bf16[2,512,768]{2,1,0:T(8,128)(2,1)} %param.33), channel_id=1, source_target_pairs={{0,1},{1,2},{2,3},{3,0},{4,5},{5,6},{6,7},{7,4},{8,9},{9,10},{10,1... | collective-permute-start | bytes 4718600 | tf_op jit(solution)/shard_map/ppermute | solution.py:21
  626.3 145.9 %collective-permute-start.1 = (bf16[2,512,768]{2,1,0:T(8,128)(2,1)}, bf16[2,512,768]{2,1,0:T(8,128)(2,1)}, u32[]{:S(2)}, u32[]{:S(2)}) collective-permute-start(bf16[2,512,768]{2,1,0:T(8,128)(2,1)} %param.33), channel_id=1, source_target_pairs={{0,3},{1,0},{2,1},{3,2},{4,7},{5,4},{6,5},{7,6},{8,11},{9,8},{10,9... | collective-permute-start | bytes 4718600 | tf_op jit(solution)/shard_map/ppermute | solution.py:26
  689.5 133.7 %collective-permute-start.2 = (bf16[2,512,768]{2,1,0:T(8,128)(2,1)}, bf16[2,512,768]{2,1,0:T(8,128)(2,1)}, u32[]{:S(2)}, u32[]{:S(2)}) collective-permute-start(bf16[2,512,768]{2,1,0:T(8,128)(2,1)} %collective-permute-done), channel_id=1, source_target_pairs={{0,1},{1,2},{2,3},{3,0},{4,5},{5,6},{6,7},{7,4},{8,9},{9,10},{10,1... | collective-permute-start | bytes 4718600 | tf_op jit(solution)/shard_map/ppermute | solution.py:21
  831.7 10.3 copy-start.56
  842.0 18.4 copy-start.55
  860.5 7.0 copy-start.58
  867.5 237.0 %all-gather.8.cloned.1.call-start = ((), (), s32[]{:S(2)}) async-start(), calls=%async_computation.14 | async-start | bytes 7864320 | tf_op jit(solution)/shard_map/all_gather | solution.py:204
  979.6 4.2 copy-start.5
  979.6 4.2 copy-start.11
  983.8 4.6 copy-start.36
  988.5 1047.5 %reduce-scatter.32.cloned.1.call-start = ((), (), s32[]{:S(2)}) async-start(), calls=%async_computation.20 | async-start | bytes 442368
  993.2 1044.3 %reduce-scatter.30.cloned.1.call-start = ((), (), s32[]{:S(2)}) async-start(), calls=%async_computation.19 | async-start | bytes 884736
  1104.5 6.3 copy-start.26
  1104.5 6.3 copy-start.54
  1201.1 18.1 copy-start.3
  1302.9 19.0 copy-start.3
  1405.5 19.0 copy-start.3
  1508.2 19.0 copy-start.3
  1610.8 19.0 copy-start.3
  1713.5 19.0 copy-start.3
  1816.1 19.0 copy-start.3
  1918.8 19.0 copy-start.3
  1942.8 10.2 slice-start
  1945.1 8.0 copy-start.22
  1945.9 7.1 slice-start.1
  1954.5 84.6 %reduce-scatter.28.cloned.1.call-start = ((), (), s32[]{:S(2)}) async-start(), calls=%async_computation.18 | async-start | bytes 2211840
  1960.1 5.5 copy-start.19
  1960.1 5.5 copy-start.21
  1977.3 8.2 copy-start.20
  1977.4 167.1 %reduce-scatter.22.cloned.1.call-start = ((), (), s32[]{:S(2)}) async-start(), calls=%async_computation.15 | async-start | bytes 7864320 | tf_op jit(solution)/shard_map/reduce_scatter | solution.py:250
  1977.6 8.0 copy-start.25
  1985.6 6.4 copy-start.23
  2005.5 252.5 %reduce-scatter.18.cloned.1.call-start = ((), (), s32[]{:S(2)}) async-start(), calls=%async_computation.12 | async-start | bytes 7864320 | tf_op jit(solution)/shard_map/reduce_scatter | solution.py:185
  2015.2 292.3 %reduce-scatter.24.cloned.1.call-start = ((), (), s32[]{:S(2)}) async-start(), calls=%async_computation.16 | async-start | bytes 2654208 | tf_op jit(solution)/shard_map/reduce_scatter | solution.py:261
  2025.5 325.8 %reduce-scatter.26.cloned.1.call-start = ((), (), s32[]{:S(2)}) async-start(), calls=%async_computation.17 | async-start | bytes 2654208 | tf_op jit(solution)/shard_map/reduce_scatter | solution.py:262
  2035.9 108.6 %copy-start.7 = (f32[1,512,768]{2,1,0:T(8,128)S(1)}, f32[1,512,768]{2,1,0:T(8,128)}, u32[]{:S(2)}) copy-start(f32[1,512,768]{2,1,0:T(8,128)} %copy-done.6) | copy-start | bytes 4718596
  2035.9 108.6 %copy-start.31 = (f32[2,512]{1,0:T(2,128)S(1)}, f32[2,512]{1,0:T(2,128)}, u32[]{:S(2)}) copy-start(f32[2,512]{1,0:T(2,128)} %copy-done.30) | copy-start | bytes 12292
  2035.9 108.6 %copy-start.39 = (f32[768]{0:T(1024)S(1)}, f32[768]{0:T(1024)}, u32[]{:S(2)}) copy-start(f32[768]{0:T(1024)} %param.22) | copy-start | bytes 9220
  2036.0 111.7 %copy-start.45 = (f32[2,512]{1,0:T(2,128)S(1)}, f32[2,512]{1,0:T(2,128)}, u32[]{:S(2)}) copy-start(f32[2,512]{1,0:T(2,128)} %copy-done.44) | copy-start | bytes 12292
  2037.5 110.3 %copy-start.41 = (f32[2,512]{1,0:T(2,128)S(1)}, f32[2,512]{1,0:T(2,128)}, u32[]{:S(2)}) copy-start(f32[2,512]{1,0:T(2,128)} %copy-done.40) | copy-start | bytes 12292
  2147.6 110.3 %copy-start.29 = (f32[2,512]{1,0:T(2,128)S(1)}, f32[2,512]{1,0:T(2,128)}, u32[]{:S(2)}) copy-start(f32[2,512]{1,0:T(2,128)} %copy-done.28) | copy-start | bytes 12292
  2147.6 110.3 %copy-start.33 = (f32[768]{0:T(1024)S(1)}, f32[768]{0:T(1024)}, u32[]{:S(2)}) copy-start(f32[768]{0:T(1024)} %param.26) | copy-start | bytes 9220
  2147.7 110.3 %copy-start.35 = (f32[2,512]{1,0:T(2,128)S(1)}, f32[2,512]{1,0:T(2,128)}, u32[]{:S(2)}) copy-start(f32[2,512]{1,0:T(2,128)} %copy-done.34) | copy-start | bytes 12292
  2147.7 110.3 %copy-start.37 = (f32[2,512]{1,0:T(2,128)S(1)}, f32[2,512]{1,0:T(2,128)}, u32[]{:S(2)}) copy-start(f32[2,512]{1,0:T(2,128)} %copy-done.36) | copy-start | bytes 12292
  2147.7 110.3 %copy-start.43 = (f32[2,512]{1,0:T(2,128)S(1)}, f32[2,512]{1,0:T(2,128)}, u32[]{:S(2)}) copy-start(f32[2,512]{1,0:T(2,128)} %copy-done.42) | copy-start | bytes 12292
  2147.7 110.3 %copy-start.52 = (f32[768]{0:T(1024)S(1)}, f32[768]{0:T(1024)}, u32[]{:S(2)}) copy-start(f32[768]{0:T(1024)} %param.31) | copy-start | bytes 9220
  2149.6 115.3 %copy-start.49 = (pred[512]{0:T(512)(128)(4,1)S(1)}, pred[512]{0:T(512)(128)(4,1)}, u32[]{:S(2)}) copy-start(pred[512]{0:T(512)(128)(4,1)} %copy-done.48) | copy-start | bytes 1540
  (33 other events, 61.8 us)
Sparse Core Ops, SparseCore 0:
  15.1 118.0 all-gather.3
  509.4 108.9 reduce-scatter.15
  624.8 206.8 all-gather.5
  867.6 111.9 reduce-scatter.19
  988.6 115.8 all-gather.7
  1107.4 32.0 reduce-scatter.31
  1954.6 33.0 reduce-scatter.29
  1991.2 40.1 reduce-scatter.27
  2033.7 110.7 reduce-scatter.21
  2146.7 111.2 reduce-scatter.17
  2261.9 42.9 reduce-scatter.23
  2308.6 42.6 reduce-scatter.25
